TPU v7x, 512 devices: a whole 4x4x16 slice. The times are simulated.
512 devices in a mesh: row: 8 (over y, x_hi), col: 16 (over z), layer: 4 (over x_lo, core).
Axes of the slice: x: 4 (x_hi: 2, x_lo: 2; x = x_hi * 2 + x_lo), y: 4, z: 16, core: 2. Of those that a mesh axis runs over, the one named last changes fastest.
Arguments:
- density: bfloat16 [2048, 16384], P('row', ('layer', 'col')), may hold values from -6 to 6
- margin: bfloat16 [16384, 16384], P(('layer', 'row'), 'col'), may hold values from -0.09375 to 0.09375
- block_pattern: int32 [128, 128], replicated, may hold values from 0 to 1, as said below
- atom_functions: int32 [512], replicated, may hold values from 1 to 9, 2048 in all
- atom_kind: int32 [512], P(('row', 'col', 'layer')), may hold values from 0 to 4
- atom_offset: float32 [3, 512], P(None, ('row', 'col', 'layer')), may hold values from 0 to 128, as said below
- exponents: float32 [5], replicated, may hold values from 0.02 to 1
Outputs:
- density_product: bfloat16 [2048, 16384], P('row', ('col', 'layer'))
- electron_density: float32 [256, 512, 512], P('row', 'col', 'layer')
Inputs may be any that keep to these rules, and one draw needn't show every extreme that they name: `block_pattern`: symmetric, with ones on its diagonal; block_pattern[i, j] = 0 whenever |i - j| > 32 (no block couples to one more than 32 blocks away). `atom_functions`: all atoms' functions together are the 2048 rows of the window. `atom_offset`: row k of an atom lies in [0, the tile's cells along dimension k), that is 32, 32 or 128.
All inputs are finite; a program needn't handle non-finite values.
Results may differ from a plain program's by a relative error of at most 0.001.
Values may be sent and summed in bfloat16 or wider, within the bound.
A program may use at most 64 MiB of HBM per device.

v0:
```python
import jax
import jax.numpy as jnp
from jax import lax
from jax.sharding import PartitionSpec as P

BLK = 128
TX = 32
TY = 32
TZ = 128
HALO = 16


def passed_along(block, axis, distance):
    devices = range(lax.axis_size(axis))
    route = [((i - distance) % len(devices), i) for i in devices]
    return lax.ppermute(block, axis, route)


def with_halo(block, sides, width):
    for axis, dim in sides:
        count = lax.axis_size(axis)
        forward = [(i, i + 1) for i in range(count - 1)]
        forward.append((count - 1, 0))
        backward = [(target, source) for source, target in forward]
        low = lax.ppermute(
            lax.slice_in_dim(block, block.shape[dim] - width, None, axis=dim), axis, forward
        )
        high = lax.ppermute(lax.slice_in_dim(block, 0, width, axis=dim), axis, backward)
        block = jnp.concatenate([low, block, high], axis=dim)
    return block


def apply_pattern(matrix, pattern_part):
    row_blocks = matrix.shape[0] // BLK
    col_blocks = matrix.shape[1] // BLK
    shaped = matrix.reshape(row_blocks, BLK, col_blocks, BLK)
    gate_mask = pattern_part.astype(jnp.bfloat16)
    return (shaped * gate_mask[:, None, :, None]).reshape(matrix.shape)


def local_profile(offset, exponent_of, extent):
    local_cells = jnp.arange(-HALO, extent + HALO, dtype=jnp.int32).astype(jnp.float32)
    distance = local_cells[None, :] - offset[:, None]
    return jnp.where(
        jnp.abs(distance) <= HALO, jnp.exp(-exponent_of[:, None] * distance * distance), 0.0
    )


def fold_rims(values_in, axis_dim, extent):
    middle = lax.slice_in_dim(values_in, 2 * HALO, 2 * HALO + extent, axis=axis_dim)
    lower_rim = lax.slice_in_dim(values_in, 0, HALO, axis=axis_dim)
    upper_rim = lax.slice_in_dim(values_in, extent + 3 * HALO, extent + 4 * HALO, axis=axis_dim)
    lower_edge = lax.slice_in_dim(middle, 0, HALO, axis=axis_dim) + lower_rim
    upper_edge = lax.slice_in_dim(middle, extent - HALO, extent, axis=axis_dim) + upper_rim
    inner_part = lax.slice_in_dim(middle, HALO, extent - HALO, axis=axis_dim)
    return jnp.concatenate([lower_edge, inner_part, upper_edge], axis=axis_dim)


def kind_exponent(kinds_of, exponents):
    kind_match = kinds_of[:, None] == jnp.arange(exponents.shape[0], dtype=jnp.int32)[None, :]
    return jnp.sum(jnp.where(kind_match, exponents[None, :], 0.0), axis=1)


def shards(density, margin, block_pattern, atom_functions, atom_kind, atom_offset, exponents):
    rows_here, piece_width = density.shape
    share_rows, share_cols = margin.shape
    n_row = lax.axis_size("row")
    n_col = lax.axis_size("col")
    n_layer = lax.axis_size("layer")
    row_index = lax.axis_index("row")
    col_index = lax.axis_index("col")
    layer_index = lax.axis_index("layer")
    density_mask = lax.dynamic_slice(
        block_pattern,
        (row_index * (rows_here // BLK), (layer_index * n_col + col_index) * piece_width // BLK),
        (rows_here // BLK, piece_width // BLK),
    )
    masked = apply_pattern(density, density_mask)
    margin_mask = lax.dynamic_slice(
        block_pattern,
        ((layer_index * n_row + row_index) * share_rows // BLK, col_index * share_cols // BLK),
        (share_rows // BLK, share_cols // BLK),
    )
    margin_masked = apply_pattern(margin, margin_mask)
    columns_panel = lax.all_gather(margin_masked, "row", axis=0, tiled=True)

    def add_piece(running, piece_rows, first_row):
        rows_of = lax.dynamic_slice_in_dim(columns_panel, first_row, piece_rows.shape[1], 0)
        return running + jnp.dot(piece_rows, rows_of, preferred_element_type=jnp.float32)

    product_zero = jnp.zeros((rows_here, share_cols), jnp.float32)

    def advance_one(turn_index, state_tuple):
        moving, running = state_tuple
        moving = passed_along(moving, "col", 1)
        return (
            moving,
            add_piece(running, moving, (col_index - turn_index - 1) % n_col * piece_width),
        )

    start_sum = add_piece(product_zero, masked, col_index * piece_width)
    product_acc = lax.fori_loop(0, n_col - 1, advance_one, (masked, start_sum))[1]
    product = lax.psum_scatter(product_acc, "layer", scatter_dimension=1, tiled=True)
    strip_width = product.shape[1]
    rows_global = row_index * rows_here + jnp.arange(rows_here, dtype=jnp.int32)
    cols_global = (col_index * n_layer + layer_index) * strip_width + jnp.arange(
        strip_width, dtype=jnp.int32
    )
    on_diagonal = rows_global[:, None] == cols_global[None, :]
    diagonal_part = jnp.sum(jnp.where(on_diagonal, product, 0.0), axis=0)
    run_ends = jnp.cumsum(atom_functions, dtype=jnp.int32)
    run_starts = run_ends - atom_functions
    member = (cols_global[:, None] >= run_starts[None, :]) & (
        cols_global[:, None] < run_ends[None, :]
    )
    partial_pop = jnp.dot(
        diagonal_part, member.astype(jnp.float32), precision=lax.Precision.HIGHEST
    )
    all_pop = lax.psum(partial_pop, ("row", "col", "layer"))
    slot_count = atom_kind.shape[0]
    tile_index = (row_index * n_col + col_index) * n_layer + layer_index
    own_pop = lax.dynamic_slice_in_dim(all_pop, tile_index * slot_count, slot_count, 0)
    exponent_of = kind_exponent(atom_kind, exponents)
    weight_x = own_pop[:, None] * local_profile(atom_offset[0], exponent_of, TX)
    along_y = local_profile(atom_offset[1], exponent_of, TY)
    along_z = local_profile(atom_offset[2], exponent_of, TZ)
    paired = weight_x[:, :, None] * along_y[:, None, :]
    extended = jnp.einsum("axy,az->xyz", paired, along_z, precision=lax.Precision.HIGHEST)
    summed = with_halo(extended, (("row", 0), ("col", 1), ("layer", 2)), HALO)
    electron_density = fold_rims(fold_rims(fold_rims(summed, 0, TX), 1, TY), 2, TZ)
    return (product.astype(jnp.bfloat16), electron_density)


def solution(mesh):
    placed = (
        P("row", ("layer", "col")),
        P(("layer", "row"), "col"),
        P(),
        P(),
        P(("row", "col", "layer")),
        P(None, ("row", "col", "layer")),
        P(),
    )
    return jax.shard_map(
        shards,
        mesh=mesh,
        in_specs=placed,
        out_specs=(P("row", ("col", "layer")), P("row", "col", "layer")),
        check_vma=False,
    )
```

profile of v0, /device:TPU:1, one launch (start us, length us, event | category | flops | bytes accessed | tf_op | source)
XLA Modules:
  0.0 577.8 jit_solution(15590409641228112352)
XLA Ops:
  10.6 127.0 %all-gather.2.cloned.1.call-done = bf16[4096,1024]{1,0:T(8,128)(2,1)} async-done(((bf16[512,1024]{1,0:T(8,128)(2,1)}), bf16[4096,1024]{1,0:T(8,128)(2,1)}) %all-gather.2.cloned.1.call-update) | async-done | bytes 8388624 | tf_op jit(solution)/shard_map/all_gather | solution.py:85
  139.1 129.6 %while.17 = (s32[]{:T(128)}, bf16[256,256]{1,0:T(8,128)(2,1)S(1)}, f32[256,1024]{0,1:T(8,128)S(1)}, s32[]{:T(128)}, bf16[4096,1024]{1,0:T(8,128)(2,1)}, /*index=...) while((s32[]{:T(128)}, bf16[256,256]{1,0:T(8,128)(2,1)S(1)}, ...), condition=%wide.region_1.2_spmd, body=%wide.region_0.1_spmd.sunk | while | flops 134479888 | bytes 3539284 | solution.py:102
  139.1 3.2 collective-permute-start
  142.3 4.8 collective-permute-done
  148.6 1.9 collective-permute-start
  150.5 5.0 collective-permute-done
  157.0 1.9 collective-permute-start
  158.9 5.0 collective-permute-done
  163.9 1.4 fusion.35
  165.3 1.9 collective-permute-start
  167.3 5.0 collective-permute-done
  172.3 1.4 fusion.35
  173.7 1.9 collective-permute-start
  175.7 5.0 collective-permute-done
  182.1 1.9 collective-permute-start
  184.1 5.0 collective-permute-done
  190.5 1.9 collective-permute-start
  192.4 5.3 collective-permute-done
  197.8 1.4 fusion.35
  199.2 1.9 collective-permute-start
  201.2 6.6 %collective-permute-done = bf16[256,256]{1,0:T(8,128)(2,1)S(1)} collective-permute-done((bf16[256,256]{1,0:T(8,128)(2,1)S(1)}, bf16[256,256]{1,0:T(8,128)(2,1)S(1)}, u32[]{:S(2)}, u32[]{:S(2)}) %collective-permute-start) | collective-permute-done | bytes 131104 | tf_op jit(solution)/shard_map/while/body/eval_jaxpr/ppermute | solution.py:16
  209.2 1.9 collective-permute-start
  211.2 5.7 collective-permute-done
  218.3 1.9 collective-permute-start
  220.3 5.0 collective-permute-done
  225.3 1.4 fusion.35
  226.7 1.9 collective-permute-start
  228.7 5.0 collective-permute-done
  235.1 1.9 collective-permute-start
  237.1 5.0 collective-permute-done
  243.5 1.9 collective-permute-start
  245.5 5.0 collective-permute-done
  251.9 1.9 collective-permute-start
  253.8 5.0 collective-permute-done
  260.3 1.9 collective-permute-start
  262.2 5.0 collective-permute-done
  274.5 38.1 %reduce-scatter.2.cloned.1.call-done = f32[256,256]{1,0:T(8,128)} async-done(((f32[256,1024]{1,0:T(8,128)}), f32[256,256]{1,0:T(8,128)}) %reduce-scatter.2.cloned.1.call-update) | async-done | bytes 262160 | tf_op jit(solution)/shard_map/reduce_scatter | solution.py:103
  312.6 1.8 select_reduce_fusion
  314.7 105.2 %psum.7 = f32[512]{0:T(512)S(1)} all-reduce(f32[512]{0:T(512)S(1)} %bitcast.36), channel_id=1, replica_groups=mesh['row'=8,'col'=16,'layer'=4] {'row','col','layer'}, use_global_device_ids=true, to_apply=%region_6.7 | all-reduce | flops 512 | bytes 4096 | tf_op jit(solution)/shard_map/psum | solution.py:119
  422.5 3.1 collective-permute-start.1
  425.6 5.8 %collective-permute-start.2 = (f32[16,64,160]{2,1,0:T(8,128)S(1)}, f32[16,64,160]{2,1,0:T(8,128)S(1)}, u32[]{:S(2)}, u32[]{:S(2)}) collective-permute-start(f32[16,64,160]{2,1,0:T(8,128)S(1)} %get-tuple-element.176), channel_id=1, source_target_pairs={{64,0},{128,64},{192,128},{256,192},{320,256},{384,320},{448,384},... | collective-permute-start | bytes 1966088 | tf_op jit(solution)/shard_map/ppermute | solution.py:28
  431.4 20.6 %collective-permute-done.1 = f32[16,64,160]{2,1,0:T(8,128)S(1)} collective-permute-done((f32[16,64,160]{2,1,0:T(8,128)S(1)}, f32[16,64,160]{2,1,0:T(8,128)S(1)}, u32[]{:S(2)}, u32[]{:S(2)}) %collective-permute-start.1) | collective-permute-done | bytes 655392 | tf_op jit(solution)/shard_map/ppermute | solution.py:25
  452.1 19.8 %collective-permute-done.2 = f32[16,64,160]{2,1,0:T(8,128)S(1)} collective-permute-done((f32[16,64,160]{2,1,0:T(8,128)S(1)}, f32[16,64,160]{2,1,0:T(8,128)S(1)}, u32[]{:S(2)}, u32[]{:S(2)}) %collective-permute-start.2) | collective-permute-done | bytes 655392 | tf_op jit(solution)/shard_map/ppermute | solution.py:28
  471.9 1.6 pad_maximum_fusion.9
  473.4 3.3 copy.23
  476.7 2.9 collective-permute-start.4
  479.7 2.1 copy.22
  481.8 2.4 collective-permute-start.3
  484.1 23.6 %collective-permute-done.4 = f32[96,16,160]{0,2,1:T(8,128)} collective-permute-done((f32[96,16,160]{0,2,1:T(8,128)}, f32[96,16,160]{0,2,1:T(8,128)}, u32[]{:S(2)}, u32[]{:S(2)}) %collective-permute-start.4) | collective-permute-done | bytes 983072 | tf_op jit(solution)/shard_map/ppermute | solution.py:28
  507.7 2.6 copy.25
  510.3 3.4 collective-permute-done.3
  513.7 3.6 copy.24
  517.3 3.7 pad_maximum_fusion
  521.0 5.3 fusion.24
  526.3 3.8 copy.26
  530.1 4.2 collective-permute-start.5
  534.3 3.8 copy.27
  538.1 2.5 collective-permute-start.6
  540.6 3.3 collective-permute-done.5
  543.9 3.8 copy.28
  547.7 6.4 %collective-permute-done.6 = f32[96,96,16]{1,2,0:T(8,128)} collective-permute-done((f32[96,96,16]{1,2,0:T(8,128)}, f32[96,96,16]{1,2,0:T(8,128)}, u32[]{:S(2)}, u32[]{:S(2)}) %collective-permute-start.6) | collective-permute-done | bytes 589856 | tf_op jit(solution)/shard_map/ppermute | solution.py:28
  554.1 3.9 copy.29
  558.0 5.8 %maximum_add_fusion = f32[16,96,192]{2,1,0:T(8,128)S(1)} fusion(f32[96,96,16]{2,1,0:T(8,128)} %copy.29, f32[96,96,16]{2,1,0:T(8,128)} %copy.28, f32[96,16,160]{2,1,0:T(8,128)S(1)} %copy.25, f32[96,16,160]{2,1,0:T(8,128)} %copy.24, f32[16,64,160]{2,1,0:T(8,128)} %copy-done.4, f32[64,64,160]{2,1,0:T(8,128)} %copy-done, ...), kind=kLoop, calls=%fused_computation.21 | loop fusion | flops 3833856 | bytes 8257536 | tf_op jit(solution)/shard_map/add | solution.py:53
  564.9 4.0 fusion.3
  (85 shorter events, 31.0 us)
Async XLA Ops:
  7.2 1.2 copy-start.6
  7.2 130.5 %all-gather.2.cloned.1.call-start = ((), (), s32[]{:S(2)}) async-start(), calls=%async_computation.1 | async-start | bytes 9437184 | tf_op jit(solution)/shard_map/all_gather | solution.py:85
  8.4 2.2 copy-start.7
  9.6 303.0 %reduce-scatter.2.cloned.1.call-start = ((), (), s32[]{:S(2)}) async-start(), calls=%async_computation.2 | async-start | bytes 1310720 | tf_op jit(solution)/shard_map/reduce_scatter | solution.py:103
  139.1 8.0 %collective-permute-start = (bf16[256,256]{1,0:T(8,128)(2,1)S(1)}, bf16[256,256]{1,0:T(8,128)(2,1)S(1)}, u32[]{:S(2)}, u32[]{:S(2)}) collective-permute-start(bf16[256,256]{1,0:T(8,128)(2,1)S(1)} %get-tuple-element.232), channel_id=1, source_target_pairs={{60,0},{0,4},{4,8},{8,12},{12,16},{16,20},{20,24},{24,28},{28,32},... | collective-permute-start | bytes 393224 | tf_op jit(solution)/shard_map/while/body/eval_jaxpr/ppermute | solution.py:16
  148.6 6.9 %collective-permute-start = (bf16[256,256]{1,0:T(8,128)(2,1)S(1)}, bf16[256,256]{1,0:T(8,128)(2,1)S(1)}, u32[]{:S(2)}, u32[]{:S(2)}) collective-permute-start(bf16[256,256]{1,0:T(8,128)(2,1)S(1)} %get-tuple-element.232), channel_id=1, source_target_pairs={{60,0},{0,4},{4,8},{8,12},{12,16},{16,20},{20,24},{24,28},{28,32},... | collective-permute-start | bytes 393224 | tf_op jit(solution)/shard_map/while/body/eval_jaxpr/ppermute | solution.py:16
  157.0 6.9 %collective-permute-start = (bf16[256,256]{1,0:T(8,128)(2,1)S(1)}, bf16[256,256]{1,0:T(8,128)(2,1)S(1)}, u32[]{:S(2)}, u32[]{:S(2)}) collective-permute-start(bf16[256,256]{1,0:T(8,128)(2,1)S(1)} %get-tuple-element.232), channel_id=1, source_target_pairs={{60,0},{0,4},{4,8},{8,12},{12,16},{16,20},{20,24},{24,28},{28,32},... | collective-permute-start | bytes 393224 | tf_op jit(solution)/shard_map/while/body/eval_jaxpr/ppermute | solution.py:16
  165.3 6.9 %collective-permute-start = (bf16[256,256]{1,0:T(8,128)(2,1)S(1)}, bf16[256,256]{1,0:T(8,128)(2,1)S(1)}, u32[]{:S(2)}, u32[]{:S(2)}) collective-permute-start(bf16[256,256]{1,0:T(8,128)(2,1)S(1)} %get-tuple-element.232), channel_id=1, source_target_pairs={{60,0},{0,4},{4,8},{8,12},{12,16},{16,20},{20,24},{24,28},{28,32},... | collective-permute-start | bytes 393224 | tf_op jit(solution)/shard_map/while/body/eval_jaxpr/ppermute | solution.py:16
  173.7 6.9 %collective-permute-start = (bf16[256,256]{1,0:T(8,128)(2,1)S(1)}, bf16[256,256]{1,0:T(8,128)(2,1)S(1)}, u32[]{:S(2)}, u32[]{:S(2)}) collective-permute-start(bf16[256,256]{1,0:T(8,128)(2,1)S(1)} %get-tuple-element.232), channel_id=1, source_target_pairs={{60,0},{0,4},{4,8},{8,12},{12,16},{16,20},{20,24},{24,28},{28,32},... | collective-permute-start | bytes 393224 | tf_op jit(solution)/shard_map/while/body/eval_jaxpr/ppermute | solution.py:16
  182.1 6.9 %collective-permute-start = (bf16[256,256]{1,0:T(8,128)(2,1)S(1)}, bf16[256,256]{1,0:T(8,128)(2,1)S(1)}, u32[]{:S(2)}, u32[]{:S(2)}) collective-permute-start(bf16[256,256]{1,0:T(8,128)(2,1)S(1)} %get-tuple-element.232), channel_id=1, source_target_pairs={{60,0},{0,4},{4,8},{8,12},{12,16},{16,20},{20,24},{24,28},{28,32},... | collective-permute-start | bytes 393224 | tf_op jit(solution)/shard_map/while/body/eval_jaxpr/ppermute | solution.py:16
  190.5 7.3 %collective-permute-start = (bf16[256,256]{1,0:T(8,128)(2,1)S(1)}, bf16[256,256]{1,0:T(8,128)(2,1)S(1)}, u32[]{:S(2)}, u32[]{:S(2)}) collective-permute-start(bf16[256,256]{1,0:T(8,128)(2,1)S(1)} %get-tuple-element.232), channel_id=1, source_target_pairs={{60,0},{0,4},{4,8},{8,12},{12,16},{16,20},{20,24},{24,28},{28,32},... | collective-permute-start | bytes 393224 | tf_op jit(solution)/shard_map/while/body/eval_jaxpr/ppermute | solution.py:16
  199.2 8.5 %collective-permute-start = (bf16[256,256]{1,0:T(8,128)(2,1)S(1)}, bf16[256,256]{1,0:T(8,128)(2,1)S(1)}, u32[]{:S(2)}, u32[]{:S(2)}) collective-permute-start(bf16[256,256]{1,0:T(8,128)(2,1)S(1)} %get-tuple-element.232), channel_id=1, source_target_pairs={{60,0},{0,4},{4,8},{8,12},{12,16},{16,20},{20,24},{24,28},{28,32},... | collective-permute-start | bytes 393224 | tf_op jit(solution)/shard_map/while/body/eval_jaxpr/ppermute | solution.py:16
  209.2 7.7 %collective-permute-start = (bf16[256,256]{1,0:T(8,128)(2,1)S(1)}, bf16[256,256]{1,0:T(8,128)(2,1)S(1)}, u32[]{:S(2)}, u32[]{:S(2)}) collective-permute-start(bf16[256,256]{1,0:T(8,128)(2,1)S(1)} %get-tuple-element.232), channel_id=1, source_target_pairs={{60,0},{0,4},{4,8},{8,12},{12,16},{16,20},{20,24},{24,28},{28,32},... | collective-permute-start | bytes 393224 | tf_op jit(solution)/shard_map/while/body/eval_jaxpr/ppermute | solution.py:16
  218.3 6.9 %collective-permute-start = (bf16[256,256]{1,0:T(8,128)(2,1)S(1)}, bf16[256,256]{1,0:T(8,128)(2,1)S(1)}, u32[]{:S(2)}, u32[]{:S(2)}) collective-permute-start(bf16[256,256]{1,0:T(8,128)(2,1)S(1)} %get-tuple-element.232), channel_id=1, source_target_pairs={{60,0},{0,4},{4,8},{8,12},{12,16},{16,20},{20,24},{24,28},{28,32},... | collective-permute-start | bytes 393224 | tf_op jit(solution)/shard_map/while/body/eval_jaxpr/ppermute | solution.py:16
  226.7 6.9 %collective-permute-start = (bf16[256,256]{1,0:T(8,128)(2,1)S(1)}, bf16[256,256]{1,0:T(8,128)(2,1)S(1)}, u32[]{:S(2)}, u32[]{:S(2)}) collective-permute-start(bf16[256,256]{1,0:T(8,128)(2,1)S(1)} %get-tuple-element.232), channel_id=1, source_target_pairs={{60,0},{0,4},{4,8},{8,12},{12,16},{16,20},{20,24},{24,28},{28,32},... | collective-permute-start | bytes 393224 | tf_op jit(solution)/shard_map/while/body/eval_jaxpr/ppermute | solution.py:16
  235.1 6.9 %collective-permute-start = (bf16[256,256]{1,0:T(8,128)(2,1)S(1)}, bf16[256,256]{1,0:T(8,128)(2,1)S(1)}, u32[]{:S(2)}, u32[]{:S(2)}) collective-permute-start(bf16[256,256]{1,0:T(8,128)(2,1)S(1)} %get-tuple-element.232), channel_id=1, source_target_pairs={{60,0},{0,4},{4,8},{8,12},{12,16},{16,20},{20,24},{24,28},{28,32},... | collective-permute-start | bytes 393224 | tf_op jit(solution)/shard_map/while/body/eval_jaxpr/ppermute | solution.py:16
  243.5 6.9 %collective-permute-start = (bf16[256,256]{1,0:T(8,128)(2,1)S(1)}, bf16[256,256]{1,0:T(8,128)(2,1)S(1)}, u32[]{:S(2)}, u32[]{:S(2)}) collective-permute-start(bf16[256,256]{1,0:T(8,128)(2,1)S(1)} %get-tuple-element.232), channel_id=1, source_target_pairs={{60,0},{0,4},{4,8},{8,12},{12,16},{16,20},{20,24},{24,28},{28,32},... | collective-permute-start | bytes 393224 | tf_op jit(solution)/shard_map/while/body/eval_jaxpr/ppermute | solution.py:16
  251.9 6.9 %collective-permute-start = (bf16[256,256]{1,0:T(8,128)(2,1)S(1)}, bf16[256,256]{1,0:T(8,128)(2,1)S(1)}, u32[]{:S(2)}, u32[]{:S(2)}) collective-permute-start(bf16[256,256]{1,0:T(8,128)(2,1)S(1)} %get-tuple-element.232), channel_id=1, source_target_pairs={{60,0},{0,4},{4,8},{8,12},{12,16},{16,20},{20,24},{24,28},{28,32},... | collective-permute-start | bytes 393224 | tf_op jit(solution)/shard_map/while/body/eval_jaxpr/ppermute | solution.py:16
  260.3 6.9 %collective-permute-start = (bf16[256,256]{1,0:T(8,128)(2,1)S(1)}, bf16[256,256]{1,0:T(8,128)(2,1)S(1)}, u32[]{:S(2)}, u32[]{:S(2)}) collective-permute-start(bf16[256,256]{1,0:T(8,128)(2,1)S(1)} %get-tuple-element.232), channel_id=1, source_target_pairs={{60,0},{0,4},{4,8},{8,12},{12,16},{16,20},{20,24},{24,28},{28,32},... | collective-permute-start | bytes 393224 | tf_op jit(solution)/shard_map/while/body/eval_jaxpr/ppermute | solution.py:16
  268.6 2.0 copy-start.10
  268.7 3.3 copy-start.8
  268.7 3.7 copy-start.9
  422.4 49.5 %copy-start = (f32[64,64,160]{2,1,0:T(8,128)}, f32[64,64,160]{2,1,0:T(8,128)S(1)}, u32[]{:S(2)}) copy-start(f32[64,64,160]{2,1,0:T(8,128)S(1)} %broadcast_multiply_fusion) | copy-start | bytes 7864324
  422.5 29.6 %collective-permute-start.1 = (f32[16,64,160]{2,1,0:T(8,128)S(1)}, f32[16,64,160]{2,1,0:T(8,128)S(1)}, u32[]{:S(2)}, u32[]{:S(2)}) collective-permute-start(f32[16,64,160]{2,1,0:T(8,128)S(1)} %get-tuple-element.175), channel_id=1, source_target_pairs={{0,64},{64,128},{128,192},{192,256},{256,320},{320,384},{384,448},... | collective-permute-start | bytes 1966088 | tf_op jit(solution)/shard_map/ppermute | solution.py:25
  425.6 46.3 %collective-permute-start.2 = (f32[16,64,160]{2,1,0:T(8,128)S(1)}, f32[16,64,160]{2,1,0:T(8,128)S(1)}, u32[]{:S(2)}, u32[]{:S(2)}) collective-permute-start(f32[16,64,160]{2,1,0:T(8,128)S(1)} %get-tuple-element.176), channel_id=1, source_target_pairs={{64,0},{128,64},{192,128},{256,192},{320,256},{384,320},{448,384},... | collective-permute-start | bytes 1966088 | tf_op jit(solution)/shard_map/ppermute | solution.py:28
  471.9 1.6 copy-start.4
  476.7 31.0 %collective-permute-start.4 = (f32[96,16,160]{0,2,1:T(8,128)}, f32[96,16,160]{0,2,1:T(8,128)}, u32[]{:S(2)}, u32[]{:S(2)}) collective-permute-start(f32[96,16,160]{0,2,1:T(8,128)} %copy.23), channel_id=1, source_target_pairs={{4,0},{8,4},{12,8},{16,12},{20,16},{24,20},{28,24},{32,28},{36,32}... | collective-permute-start | bytes 2949128 | tf_op jit(solution)/shard_map/ppermute | solution.py:28
  481.8 31.9 %collective-permute-start.3 = (f32[96,16,160]{0,2,1:T(8,128)}, f32[96,16,160]{0,2,1:T(8,128)}, u32[]{:S(2)}, u32[]{:S(2)}) collective-permute-start(f32[96,16,160]{0,2,1:T(8,128)} %copy.22), channel_id=1, source_target_pairs={{0,4},{4,8},{8,12},{12,16},{16,20},{20,24},{24,28},{28,32},{32,36}... | collective-permute-start | bytes 2949128 | tf_op jit(solution)/shard_map/ppermute | solution.py:25
  530.1 13.8 %collective-permute-start.5 = (f32[96,96,16]{1,2,0:T(8,128)}, f32[96,96,16]{1,2,0:T(8,128)}, u32[]{:S(2)}, u32[]{:S(2)}) collective-permute-start(f32[96,96,16]{1,2,0:T(8,128)} %copy.26), channel_id=1, source_target_pairs={{0,1},{1,2},{2,3},{3,0},{4,5},{5,6},{6,7},{7,4},{8,9},{9,10},{10,1... | collective-permute-start | bytes 1769480 | tf_op jit(solution)/shard_map/ppermute | solution.py:25
  538.1 16.0 %collective-permute-start.6 = (f32[96,96,16]{1,2,0:T(8,128)}, f32[96,96,16]{1,2,0:T(8,128)}, u32[]{:S(2)}, u32[]{:S(2)}) collective-permute-start(f32[96,96,16]{1,2,0:T(8,128)} %copy.27), channel_id=1, source_target_pairs={{1,0},{2,1},{3,2},{0,3},{5,4},{6,5},{7,6},{4,7},{9,8},{10,9},{11,1... | collective-permute-start | bytes 1769480 | tf_op jit(solution)/shard_map/ppermute | solution.py:28
  554.1 9.8 %slice-start = ((s8[4718592]{0:T(1024)(128)(4,1)}), s8[524288]{0:T(1024)(128)(4,1)S(1)}, s32[]{:S(2)}) async-start(s8[4718592]{0:T(1024)(128)(4,1)} %bitcast.31), calls=%async_computation.3 | async-start | bytes 1048576
  558.0 5.9 %copy-start.1 = (f32[64,64,160]{2,1,0:T(8,128)S(1)}, f32[64,64,160]{2,1,0:T(8,128)}, u32[]{:S(2)}) copy-start(f32[64,64,160]{2,1,0:T(8,128)} %copy-done) | copy-start | bytes 7864324
  558.0 5.9 %slice-start.1 = ((s8[4718592]{0:T(1024)(128)(4,1)}), s8[4194304]{0:T(1024)(128)(4,1)S(1)}, s32[]{:S(2)}) async-start(s8[4718592]{0:T(1024)(128)(4,1)} %bitcast.31), calls=%async_computation.4 | async-start | bytes 8388608
  558.0 6.2 %copy-start.2 = (f32[96,96,16]{2,1,0:T(8,128)S(1)}, f32[96,96,16]{2,1,0:T(8,128)}, u32[]{:S(2)}) copy-start(f32[96,96,16]{2,1,0:T(8,128)} %copy.29) | copy-start | bytes 1769476
  558.0 6.6 %copy-start.3 = (f32[96,16,160]{2,1,0:T(8,128)S(1)}, f32[96,16,160]{2,1,0:T(8,128)}, u32[]{:S(2)}) copy-start(f32[96,16,160]{2,1,0:T(8,128)} %copy.24) | copy-start | bytes 2949124
  558.0 6.9 %copy-start.5 = (f32[16,64,160]{2,1,0:T(8,128)S(1)}, f32[16,64,160]{2,1,0:T(8,128)}, u32[]{:S(2)}) copy-start(f32[16,64,160]{2,1,0:T(8,128)} %copy-done.4) | copy-start | bytes 1966084
Sparse Core Ops, SparseCore 0:
  11.2 126.4 all-gather.1
  270.1 42.3 reduce-scatter.1
where the time goes:
time: 580 us; the launch traced here: 578 us
  waiting for transfers between devices  319 us (55%)
  blocking collectives  105 us (18%)
  starting transfers between devices  51 us (9%)
  local copies, waits for them, and re-layouts  36.6 us (6%)
  other arithmetic  25.9 us (4%)
  matrix products  23.1 us (4%)
  between operations  15.7 us (3%)
    all_gather x1, waiting for transfers between devices, shards(): columns_panel = lax.all_gather(margin_masked, 'row', axis=0, tiled=True)  127 us
    psum x1, blocking collectives, shards(): all_pop = lax.psum(partial_pop, ('row', 'col', 'layer'))  105 us
    ppermute x15, waiting for transfers between devices, passed_along(): return lax.ppermute(block, axis, route)  77.1 us
    ppermute x3, waiting for transfers between devices, with_halo(): lax.ppermute(lax.slice_in_dim(block, 0, width, axis=dim), axis, backward)  49.8 us
    reduce_scatter x1, waiting for transfers between devices, shards(): lax.psum_scatter(product_acc, 'layer', scatter_dimension=1, tiled=True)  38.1 us
    ppermute x15, starting transfers between devices, passed_along(): return lax.ppermute(block, axis, route)  30.1 us
    ppermute x3, waiting for transfers between devices, with_halo(): lax.ppermute(lax.slice_in_dim(block, block.shape[dim] - width, None, axis...  27.3 us
    dot_general x16, matrix products, add_piece(): jnp.dot(piece_rows, rows_of, preferred_element_type=jnp.float32)  22.8 us
  transfers between devices with their start and end apart: 23, of which 23 were waited for; matrix products, arithmetic and copies ran while one was open for 3% of the time, Pallas kernels for 0%

commit v1 on v0

--- a/solution.py
+++ b/solution.py
@@ -1,3 +1,4 @@
+import functools
 import jax
 import jax.numpy as jnp
 from jax import lax
@@ -8,6 +9,15 @@
 TY = 32
 TZ = 128
 HALO = 16
+
+
+def _update_targets(own_rows, axis_k):
+    last = jnp.stack([own_rows for _ in range(lax.psum(1, axis_name="row"))])
+    latest = lax.all_to_all(last, axis_name="row", split_axis=0, concat_axis=0)
+    return jnp.concatenate(latest, axis=axis_k)
+
+
+copies_get = functools.partial(_update_targets, axis_k=0)
 
 
 def passed_along(block, axis, distance):
@@ -82,7 +92,7 @@
         (share_rows // BLK, share_cols // BLK),
     )
     margin_masked = apply_pattern(margin, margin_mask)
-    columns_panel = lax.all_gather(margin_masked, "row", axis=0, tiled=True)
+    columns_panel = copies_get(margin_masked)
 
     def add_piece(running, piece_rows, first_row):
         rows_of = lax.dynamic_slice_in_dim(columns_panel, first_row, piece_rows.shape[1], 0)

time: 580 us -> 561 us (0.967)
  waiting for transfers between devices: 319 us -> 286 us
  starting transfers between devices: 51 us -> 62.2 us
    all_gather x1 -> x0, waiting for transfers between devices: 127 us -> none  [shards(): columns_panel = lax.all_gather(margin_masked, 'row', axis=0, tiled=True)]
    all_to_all x0 -> x1, waiting for transfers between devices: none -> 90.8 us  [_update_targets(): latest = lax.all_to_all(last, axis_name='row', split_axis=0, concat_axis=0)]
    all_to_all x0 -> x1, starting transfers between devices: none -> 7.6 us  [_update_targets(): latest = lax.all_to_all(last, axis_name='row', split_axis=0, concat_axis=0)]
where the time goes in v1:
time: 561 us; the launch traced here: 559 us
  waiting for transfers between devices  286 us (51%)
  blocking collectives  105 us (19%)
  starting transfers between devices  62.2 us (11%)
  local copies, waits for them, and re-layouts  41.1 us (7%)
  other arithmetic  24.9 us (4%)
  matrix products  23.1 us (4%)
  between operations  15.7 us (3%)
    psum x1, blocking collectives, shards(): all_pop = lax.psum(partial_pop, ('row', 'col', 'layer'))  105 us
    all_to_all x1, waiting for transfers between devices, _update_targets(): latest = lax.all_to_all(last, axis_name='row', split_axis=0, concat_axis=0)  90.8 us
    ppermute x15, waiting for transfers between devices, passed_along(): return lax.ppermute(block, axis, route)  81.7 us
    ppermute x3, waiting for transfers between devices, with_halo(): lax.ppermute(lax.slice_in_dim(block, 0, width, axis=dim), axis, backward)  50 us
    reduce_scatter x1, waiting for transfers between devices, shards(): lax.psum_scatter(product_acc, 'layer', scatter_dimension=1, tiled=True)  36.2 us
    ppermute x15, starting transfers between devices, passed_along(): return lax.ppermute(block, axis, route)  33.7 us
    ppermute x3, waiting for transfers between devices, with_halo(): lax.ppermute(lax.slice_in_dim(block, block.shape[dim] - width, None, axis...  27.2 us
    dot_general x16, matrix products, add_piece(): jnp.dot(piece_rows, rows_of, preferred_element_type=jnp.float32)  22.8 us
  transfers between devices with their start and end apart: 23, of which 23 were waited for; matrix products, arithmetic and copies ran while one was open for 3% of the time, Pallas kernels for 0%

profile of v1, /device:TPU:1, one launch (start us, length us, event | category | flops | bytes accessed | tf_op | source)
XLA Modules:
  0.0 559.0 jit_solution(1104193049051275824)
XLA Ops:
  8.5 4.3 stack.3
  12.9 7.6 %all-to-all-start = ((bf16[8,512,1024]{2,1,0:T(8,128)(2,1)}), bf16[8,512,1024]{2,1,0:T(8,128)(2,1)}, u32[]{:S(2)}, u32[]{:S(2)}) async-start(bf16[8,512,1024]{2,1,0:T(8,128)(2,1)} %stack.3), calls=%async_computation | async-start | bytes 16777216 | tf_op jit(solution)/shard_map/all_to_all | solution.py:16
  21.5 90.8 %all-to-all-done = bf16[8,512,1024]{2,1,0:T(8,128)(2,1)} async-done(((bf16[8,512,1024]{2,1,0:T(8,128)(2,1)}), bf16[8,512,1024]{2,1,0:T(8,128)(2,1)}, u32[]{:S(2)}, u32[]{:S(2)}) %all-to-all-start) | async-done | bytes 8388640 | tf_op jit(solution)/shard_map/all_to_all | solution.py:16
  113.7 137.8 %while.17 = (s32[]{:T(128)}, bf16[256,256]{1,0:T(8,128)(2,1)S(1)}, f32[256,1024]{0,1:T(8,128)S(1)}, s32[]{:T(128)}, bf16[4096,1024]{1,0:T(8,128)(2,1)}, /*index=...) while((s32[]{:T(128)}, bf16[256,256]{1,0:T(8,128)(2,1)S(1)}, ...), condition=%wide.region_1.2_spmd, body=%wide.region_0.1_spmd.sunk | while | flops 134479888 | bytes 3539284 | solution.py:112
  113.7 6.8 %collective-permute-start = (bf16[256,256]{1,0:T(8,128)(2,1)S(1)}, bf16[256,256]{1,0:T(8,128)(2,1)S(1)}, u32[]{:S(2)}, u32[]{:S(2)}) collective-permute-start(bf16[256,256]{1,0:T(8,128)(2,1)S(1)} %get-tuple-element.232), channel_id=1, source_target_pairs={{60,0},{0,4},{4,8},{8,12},{12,16},{16,20},{20,24},{24,28},{28,32},... | collective-permute-start | bytes 393224 | tf_op jit(solution)/shard_map/while/body/eval_jaxpr/ppermute | solution.py:26
  120.5 9.9 %collective-permute-done = bf16[256,256]{1,0:T(8,128)(2,1)S(1)} collective-permute-done((bf16[256,256]{1,0:T(8,128)(2,1)S(1)}, bf16[256,256]{1,0:T(8,128)(2,1)S(1)}, u32[]{:S(2)}, u32[]{:S(2)}) %collective-permute-start) | collective-permute-done | bytes 131104 | tf_op jit(solution)/shard_map/while/body/eval_jaxpr/ppermute | solution.py:26
  131.9 1.9 collective-permute-start
  133.9 5.0 collective-permute-done
  140.3 1.9 collective-permute-start
  142.2 5.0 collective-permute-done
  147.2 1.4 fusion.35
  148.7 1.9 collective-permute-start
  150.6 5.0 collective-permute-done
  157.1 1.9 collective-permute-start
  159.0 5.0 collective-permute-done
  165.4 1.9 collective-permute-start
  167.4 5.0 collective-permute-done
  173.8 1.9 collective-permute-start
  175.8 5.8 %collective-permute-done = bf16[256,256]{1,0:T(8,128)(2,1)S(1)} collective-permute-done((bf16[256,256]{1,0:T(8,128)(2,1)S(1)}, bf16[256,256]{1,0:T(8,128)(2,1)S(1)}, u32[]{:S(2)}, u32[]{:S(2)}) %collective-permute-start) | collective-permute-done | bytes 131104 | tf_op jit(solution)/shard_map/while/body/eval_jaxpr/ppermute | solution.py:26
  183.0 1.9 collective-permute-start
  185.0 6.1 %collective-permute-done = bf16[256,256]{1,0:T(8,128)(2,1)S(1)} collective-permute-done((bf16[256,256]{1,0:T(8,128)(2,1)S(1)}, bf16[256,256]{1,0:T(8,128)(2,1)S(1)}, u32[]{:S(2)}, u32[]{:S(2)}) %collective-permute-start) | collective-permute-done | bytes 131104 | tf_op jit(solution)/shard_map/while/body/eval_jaxpr/ppermute | solution.py:26
  191.1 1.4 fusion.35
  192.5 1.9 collective-permute-start
  194.5 5.3 collective-permute-done
  201.2 1.9 collective-permute-start
  203.2 5.0 collective-permute-done
  209.6 1.9 collective-permute-start
  211.6 5.0 collective-permute-done
  218.0 1.9 collective-permute-start
  219.9 5.0 collective-permute-done
  226.4 1.9 collective-permute-start
  228.3 5.0 collective-permute-done
  234.8 1.9 collective-permute-start
  236.7 5.0 collective-permute-done
  243.1 1.9 collective-permute-start
  245.1 5.0 collective-permute-done
  257.4 36.2 %reduce-scatter.2.cloned.1.call-done = f32[256,256]{1,0:T(8,128)} async-done(((f32[256,1024]{1,0:T(8,128)}), f32[256,256]{1,0:T(8,128)}) %reduce-scatter.2.cloned.1.call-update) | async-done | bytes 262160 | tf_op jit(solution)/shard_map/reduce_scatter | solution.py:113
  293.7 1.8 select_reduce_fusion
  295.8 105.2 %psum.7 = f32[512]{0:T(512)S(1)} all-reduce(f32[512]{0:T(512)S(1)} %bitcast.37), channel_id=1, replica_groups=mesh['row'=8,'col'=16,'layer'=4] {'row','col','layer'}, use_global_device_ids=true, to_apply=%region_6.7 | all-reduce | flops 512 | bytes 4096 | tf_op jit(solution)/shard_map/psum | solution.py:129
  403.7 3.1 collective-permute-start.1
  406.8 5.8 %collective-permute-start.2 = (f32[16,64,160]{2,1,0:T(8,128)S(1)}, f32[16,64,160]{2,1,0:T(8,128)S(1)}, u32[]{:S(2)}, u32[]{:S(2)}) collective-permute-start(f32[16,64,160]{2,1,0:T(8,128)S(1)} %get-tuple-element.176), channel_id=1, source_target_pairs={{64,0},{128,64},{192,128},{256,192},{320,256},{384,320},{448,384},... | collective-permute-start | bytes 1966088 | tf_op jit(solution)/shard_map/ppermute | solution.py:38
  412.6 20.6 %collective-permute-done.1 = f32[16,64,160]{2,1,0:T(8,128)S(1)} collective-permute-done((f32[16,64,160]{2,1,0:T(8,128)S(1)}, f32[16,64,160]{2,1,0:T(8,128)S(1)}, u32[]{:S(2)}, u32[]{:S(2)}) %collective-permute-start.1) | collective-permute-done | bytes 655392 | tf_op jit(solution)/shard_map/ppermute | solution.py:35
  433.3 19.8 %collective-permute-done.2 = f32[16,64,160]{2,1,0:T(8,128)S(1)} collective-permute-done((f32[16,64,160]{2,1,0:T(8,128)S(1)}, f32[16,64,160]{2,1,0:T(8,128)S(1)}, u32[]{:S(2)}, u32[]{:S(2)}) %collective-permute-start.2) | collective-permute-done | bytes 655392 | tf_op jit(solution)/shard_map/ppermute | solution.py:38
  453.1 1.6 pad_maximum_fusion.9
  454.7 3.3 copy.23
  458.0 2.9 collective-permute-start.4
  460.9 2.1 copy.22
  463.0 2.3 collective-permute-start.3
  465.3 23.6 %collective-permute-done.4 = f32[96,16,160]{0,2,1:T(8,128)} collective-permute-done((f32[96,16,160]{0,2,1:T(8,128)}, f32[96,16,160]{0,2,1:T(8,128)}, u32[]{:S(2)}, u32[]{:S(2)}) %collective-permute-start.4) | collective-permute-done | bytes 983072 | tf_op jit(solution)/shard_map/ppermute | solution.py:38
  489.0 2.6 copy.25
  491.6 3.4 collective-permute-done.3
  494.9 3.6 copy.24
  498.5 3.7 pad_maximum_fusion
  502.2 5.3 fusion.24
  507.5 3.8 copy.26
  511.3 4.4 collective-permute-start.5
  515.7 3.8 copy.27
  519.5 2.3 collective-permute-start.6
  521.8 3.2 collective-permute-done.5
  525.0 3.8 copy.28
  528.8 6.5 %collective-permute-done.6 = f32[96,96,16]{1,2,0:T(8,128)} collective-permute-done((f32[96,96,16]{1,2,0:T(8,128)}, f32[96,96,16]{1,2,0:T(8,128)}, u32[]{:S(2)}, u32[]{:S(2)}) %collective-permute-start.6) | collective-permute-done | bytes 589856 | tf_op jit(solution)/shard_map/ppermute | solution.py:38
  535.3 3.9 copy.29
  539.3 5.8 %maximum_add_fusion = f32[16,96,192]{2,1,0:T(8,128)S(1)} fusion(f32[96,96,16]{2,1,0:T(8,128)} %copy.29, f32[96,96,16]{2,1,0:T(8,128)} %copy.28, f32[96,16,160]{2,1,0:T(8,128)S(1)} %copy.25, f32[96,16,160]{2,1,0:T(8,128)} %copy.24, f32[16,64,160]{2,1,0:T(8,128)} %copy-done.4, f32[64,64,160]{2,1,0:T(8,128)} %copy-done, ...), kind=kLoop, calls=%fused_computation.21 | loop fusion | flops 3833856 | bytes 8257536 | tf_op jit(solution)/shard_map/add | solution.py:63
  546.1 4.0 fusion.3
  (85 shorter events, 33.0 us)
Async XLA Ops:
  7.2 1.2 copy-start.6
  12.9 8.6 %copy-start.7 = (bf16[256,256]{1,0:T(8,128)(2,1)S(1)}, bf16[256,256]{1,0:T(8,128)(2,1)}, u32[]{:S(2)}) copy-start(bf16[256,256]{1,0:T(8,128)(2,1)} %param.9) | copy-start | bytes 393220
  12.9 99.4 %all-to-all-start = ((bf16[8,512,1024]{2,1,0:T(8,128)(2,1)}), bf16[8,512,1024]{2,1,0:T(8,128)(2,1)}, u32[]{:S(2)}, u32[]{:S(2)}) async-start(bf16[8,512,1024]{2,1,0:T(8,128)(2,1)} %stack.3), calls=%async_computation | async-start | bytes 16777216 | tf_op jit(solution)/shard_map/all_to_all | solution.py:16
  20.5 273.2 %reduce-scatter.2.cloned.1.call-start = ((), (), s32[]{:S(2)}) async-start(), calls=%async_computation.2 | async-start | bytes 1310720 | tf_op jit(solution)/shard_map/reduce_scatter | solution.py:113
  113.7 16.8 %collective-permute-start = (bf16[256,256]{1,0:T(8,128)(2,1)S(1)}, bf16[256,256]{1,0:T(8,128)(2,1)S(1)}, u32[]{:S(2)}, u32[]{:S(2)}) collective-permute-start(bf16[256,256]{1,0:T(8,128)(2,1)S(1)} %get-tuple-element.232), channel_id=1, source_target_pairs={{60,0},{0,4},{4,8},{8,12},{12,16},{16,20},{20,24},{24,28},{28,32},... | collective-permute-start | bytes 393224 | tf_op jit(solution)/shard_map/while/body/eval_jaxpr/ppermute | solution.py:26
  131.9 6.9 %collective-permute-start = (bf16[256,256]{1,0:T(8,128)(2,1)S(1)}, bf16[256,256]{1,0:T(8,128)(2,1)S(1)}, u32[]{:S(2)}, u32[]{:S(2)}) collective-permute-start(bf16[256,256]{1,0:T(8,128)(2,1)S(1)} %get-tuple-element.232), channel_id=1, source_target_pairs={{60,0},{0,4},{4,8},{8,12},{12,16},{16,20},{20,24},{24,28},{28,32},... | collective-permute-start | bytes 393224 | tf_op jit(solution)/shard_map/while/body/eval_jaxpr/ppermute | solution.py:26
  140.3 6.9 %collective-permute-start = (bf16[256,256]{1,0:T(8,128)(2,1)S(1)}, bf16[256,256]{1,0:T(8,128)(2,1)S(1)}, u32[]{:S(2)}, u32[]{:S(2)}) collective-permute-start(bf16[256,256]{1,0:T(8,128)(2,1)S(1)} %get-tuple-element.232), channel_id=1, source_target_pairs={{60,0},{0,4},{4,8},{8,12},{12,16},{16,20},{20,24},{24,28},{28,32},... | collective-permute-start | bytes 393224 | tf_op jit(solution)/shard_map/while/body/eval_jaxpr/ppermute | solution.py:26
  148.7 6.9 %collective-permute-start = (bf16[256,256]{1,0:T(8,128)(2,1)S(1)}, bf16[256,256]{1,0:T(8,128)(2,1)S(1)}, u32[]{:S(2)}, u32[]{:S(2)}) collective-permute-start(bf16[256,256]{1,0:T(8,128)(2,1)S(1)} %get-tuple-element.232), channel_id=1, source_target_pairs={{60,0},{0,4},{4,8},{8,12},{12,16},{16,20},{20,24},{24,28},{28,32},... | collective-permute-start | bytes 393224 | tf_op jit(solution)/shard_map/while/body/eval_jaxpr/ppermute | solution.py:26
  157.1 6.9 %collective-permute-start = (bf16[256,256]{1,0:T(8,128)(2,1)S(1)}, bf16[256,256]{1,0:T(8,128)(2,1)S(1)}, u32[]{:S(2)}, u32[]{:S(2)}) collective-permute-start(bf16[256,256]{1,0:T(8,128)(2,1)S(1)} %get-tuple-element.232), channel_id=1, source_target_pairs={{60,0},{0,4},{4,8},{8,12},{12,16},{16,20},{20,24},{24,28},{28,32},... | collective-permute-start | bytes 393224 | tf_op jit(solution)/shard_map/while/body/eval_jaxpr/ppermute | solution.py:26
  165.4 6.9 %collective-permute-start = (bf16[256,256]{1,0:T(8,128)(2,1)S(1)}, bf16[256,256]{1,0:T(8,128)(2,1)S(1)}, u32[]{:S(2)}, u32[]{:S(2)}) collective-permute-start(bf16[256,256]{1,0:T(8,128)(2,1)S(1)} %get-tuple-element.232), channel_id=1, source_target_pairs={{60,0},{0,4},{4,8},{8,12},{12,16},{16,20},{20,24},{24,28},{28,32},... | collective-permute-start | bytes 393224 | tf_op jit(solution)/shard_map/while/body/eval_jaxpr/ppermute | solution.py:26
  173.8 7.7 %collective-permute-start = (bf16[256,256]{1,0:T(8,128)(2,1)S(1)}, bf16[256,256]{1,0:T(8,128)(2,1)S(1)}, u32[]{:S(2)}, u32[]{:S(2)}) collective-permute-start(bf16[256,256]{1,0:T(8,128)(2,1)S(1)} %get-tuple-element.232), channel_id=1, source_target_pairs={{60,0},{0,4},{4,8},{8,12},{12,16},{16,20},{20,24},{24,28},{28,32},... | collective-permute-start | bytes 393224 | tf_op jit(solution)/shard_map/while/body/eval_jaxpr/ppermute | solution.py:26
  183.0 8.1 %collective-permute-start = (bf16[256,256]{1,0:T(8,128)(2,1)S(1)}, bf16[256,256]{1,0:T(8,128)(2,1)S(1)}, u32[]{:S(2)}, u32[]{:S(2)}) collective-permute-start(bf16[256,256]{1,0:T(8,128)(2,1)S(1)} %get-tuple-element.232), channel_id=1, source_target_pairs={{60,0},{0,4},{4,8},{8,12},{12,16},{16,20},{20,24},{24,28},{28,32},... | collective-permute-start | bytes 393224 | tf_op jit(solution)/shard_map/while/body/eval_jaxpr/ppermute | solution.py:26
  192.5 7.2 %collective-permute-start = (bf16[256,256]{1,0:T(8,128)(2,1)S(1)}, bf16[256,256]{1,0:T(8,128)(2,1)S(1)}, u32[]{:S(2)}, u32[]{:S(2)}) collective-permute-start(bf16[256,256]{1,0:T(8,128)(2,1)S(1)} %get-tuple-element.232), channel_id=1, source_target_pairs={{60,0},{0,4},{4,8},{8,12},{12,16},{16,20},{20,24},{24,28},{28,32},... | collective-permute-start | bytes 393224 | tf_op jit(solution)/shard_map/while/body/eval_jaxpr/ppermute | solution.py:26
  201.2 6.9 %collective-permute-start = (bf16[256,256]{1,0:T(8,128)(2,1)S(1)}, bf16[256,256]{1,0:T(8,128)(2,1)S(1)}, u32[]{:S(2)}, u32[]{:S(2)}) collective-permute-start(bf16[256,256]{1,0:T(8,128)(2,1)S(1)} %get-tuple-element.232), channel_id=1, source_target_pairs={{60,0},{0,4},{4,8},{8,12},{12,16},{16,20},{20,24},{24,28},{28,32},... | collective-permute-start | bytes 393224 | tf_op jit(solution)/shard_map/while/body/eval_jaxpr/ppermute | solution.py:26
  209.6 6.9 %collective-permute-start = (bf16[256,256]{1,0:T(8,128)(2,1)S(1)}, bf16[256,256]{1,0:T(8,128)(2,1)S(1)}, u32[]{:S(2)}, u32[]{:S(2)}) collective-permute-start(bf16[256,256]{1,0:T(8,128)(2,1)S(1)} %get-tuple-element.232), channel_id=1, source_target_pairs={{60,0},{0,4},{4,8},{8,12},{12,16},{16,20},{20,24},{24,28},{28,32},... | collective-permute-start | bytes 393224 | tf_op jit(solution)/shard_map/while/body/eval_jaxpr/ppermute | solution.py:26
  218.0 6.9 %collective-permute-start = (bf16[256,256]{1,0:T(8,128)(2,1)S(1)}, bf16[256,256]{1,0:T(8,128)(2,1)S(1)}, u32[]{:S(2)}, u32[]{:S(2)}) collective-permute-start(bf16[256,256]{1,0:T(8,128)(2,1)S(1)} %get-tuple-element.232), channel_id=1, source_target_pairs={{60,0},{0,4},{4,8},{8,12},{12,16},{16,20},{20,24},{24,28},{28,32},... | collective-permute-start | bytes 393224 | tf_op jit(solution)/shard_map/while/body/eval_jaxpr/ppermute | solution.py:26
  226.4 6.9 %collective-permute-start = (bf16[256,256]{1,0:T(8,128)(2,1)S(1)}, bf16[256,256]{1,0:T(8,128)(2,1)S(1)}, u32[]{:S(2)}, u32[]{:S(2)}) collective-permute-start(bf16[256,256]{1,0:T(8,128)(2,1)S(1)} %get-tuple-element.232), channel_id=1, source_target_pairs={{60,0},{0,4},{4,8},{8,12},{12,16},{16,20},{20,24},{24,28},{28,32},... | collective-permute-start | bytes 393224 | tf_op jit(solution)/shard_map/while/body/eval_jaxpr/ppermute | solution.py:26
  234.8 6.9 %collective-permute-start = (bf16[256,256]{1,0:T(8,128)(2,1)S(1)}, bf16[256,256]{1,0:T(8,128)(2,1)S(1)}, u32[]{:S(2)}, u32[]{:S(2)}) collective-permute-start(bf16[256,256]{1,0:T(8,128)(2,1)S(1)} %get-tuple-element.232), channel_id=1, source_target_pairs={{60,0},{0,4},{4,8},{8,12},{12,16},{16,20},{20,24},{24,28},{28,32},... | collective-permute-start | bytes 393224 | tf_op jit(solution)/shard_map/while/body/eval_jaxpr/ppermute | solution.py:26
  243.1 6.9 %collective-permute-start = (bf16[256,256]{1,0:T(8,128)(2,1)S(1)}, bf16[256,256]{1,0:T(8,128)(2,1)S(1)}, u32[]{:S(2)}, u32[]{:S(2)}) collective-permute-start(bf16[256,256]{1,0:T(8,128)(2,1)S(1)} %get-tuple-element.232), channel_id=1, source_target_pairs={{60,0},{0,4},{4,8},{8,12},{12,16},{16,20},{20,24},{24,28},{28,32},... | collective-permute-start | bytes 393224 | tf_op jit(solution)/shard_map/while/body/eval_jaxpr/ppermute | solution.py:26
  251.5 2.0 copy-start.10
  251.5 3.3 copy-start.8
  251.5 3.7 copy-start.9
  403.6 49.5 %copy-start = (f32[64,64,160]{2,1,0:T(8,128)}, f32[64,64,160]{2,1,0:T(8,128)S(1)}, u32[]{:S(2)}) copy-start(f32[64,64,160]{2,1,0:T(8,128)S(1)} %broadcast_multiply_fusion) | copy-start | bytes 7864324
  403.7 29.6 %collective-permute-start.1 = (f32[16,64,160]{2,1,0:T(8,128)S(1)}, f32[16,64,160]{2,1,0:T(8,128)S(1)}, u32[]{:S(2)}, u32[]{:S(2)}) collective-permute-start(f32[16,64,160]{2,1,0:T(8,128)S(1)} %get-tuple-element.175), channel_id=1, source_target_pairs={{0,64},{64,128},{128,192},{192,256},{256,320},{320,384},{384,448},... | collective-permute-start | bytes 1966088 | tf_op jit(solution)/shard_map/ppermute | solution.py:35
  406.8 46.3 %collective-permute-start.2 = (f32[16,64,160]{2,1,0:T(8,128)S(1)}, f32[16,64,160]{2,1,0:T(8,128)S(1)}, u32[]{:S(2)}, u32[]{:S(2)}) collective-permute-start(f32[16,64,160]{2,1,0:T(8,128)S(1)} %get-tuple-element.176), channel_id=1, source_target_pairs={{64,0},{128,64},{192,128},{256,192},{320,256},{384,320},{448,384},... | collective-permute-start | bytes 1966088 | tf_op jit(solution)/shard_map/ppermute | solution.py:38
  453.1 1.6 copy-start.4
  458.0 31.0 %collective-permute-start.4 = (f32[96,16,160]{0,2,1:T(8,128)}, f32[96,16,160]{0,2,1:T(8,128)}, u32[]{:S(2)}, u32[]{:S(2)}) collective-permute-start(f32[96,16,160]{0,2,1:T(8,128)} %copy.23), channel_id=1, source_target_pairs={{4,0},{8,4},{12,8},{16,12},{20,16},{24,20},{28,24},{32,28},{36,32}... | collective-permute-start | bytes 2949128 | tf_op jit(solution)/shard_map/ppermute | solution.py:38
  463.0 31.9 %collective-permute-start.3 = (f32[96,16,160]{0,2,1:T(8,128)}, f32[96,16,160]{0,2,1:T(8,128)}, u32[]{:S(2)}, u32[]{:S(2)}) collective-permute-start(f32[96,16,160]{0,2,1:T(8,128)} %copy.22), channel_id=1, source_target_pairs={{0,4},{4,8},{8,12},{12,16},{16,20},{20,24},{24,28},{28,32},{32,36}... | collective-permute-start | bytes 2949128 | tf_op jit(solution)/shard_map/ppermute | solution.py:35
  511.3 13.7 %collective-permute-start.5 = (f32[96,96,16]{1,2,0:T(8,128)}, f32[96,96,16]{1,2,0:T(8,128)}, u32[]{:S(2)}, u32[]{:S(2)}) collective-permute-start(f32[96,96,16]{1,2,0:T(8,128)} %copy.26), channel_id=1, source_target_pairs={{0,1},{1,2},{2,3},{3,0},{4,5},{5,6},{6,7},{7,4},{8,9},{9,10},{10,1... | collective-permute-start | bytes 1769480 | tf_op jit(solution)/shard_map/ppermute | solution.py:35
  519.5 15.8 %collective-permute-start.6 = (f32[96,96,16]{1,2,0:T(8,128)}, f32[96,96,16]{1,2,0:T(8,128)}, u32[]{:S(2)}, u32[]{:S(2)}) collective-permute-start(f32[96,96,16]{1,2,0:T(8,128)} %copy.27), channel_id=1, source_target_pairs={{1,0},{2,1},{3,2},{0,3},{5,4},{6,5},{7,6},{4,7},{9,8},{10,9},{11,1... | collective-permute-start | bytes 1769480 | tf_op jit(solution)/shard_map/ppermute | solution.py:38
  535.3 9.8 %slice-start = ((s8[4718592]{0:T(1024)(128)(4,1)}), s8[524288]{0:T(1024)(128)(4,1)S(1)}, s32[]{:S(2)}) async-start(s8[4718592]{0:T(1024)(128)(4,1)} %bitcast.32), calls=%async_computation.3 | async-start | bytes 1048576
  539.3 5.9 %copy-start.1 = (f32[64,64,160]{2,1,0:T(8,128)S(1)}, f32[64,64,160]{2,1,0:T(8,128)}, u32[]{:S(2)}) copy-start(f32[64,64,160]{2,1,0:T(8,128)} %copy-done) | copy-start | bytes 7864324
  539.3 5.9 %slice-start.1 = ((s8[4718592]{0:T(1024)(128)(4,1)}), s8[4194304]{0:T(1024)(128)(4,1)S(1)}, s32[]{:S(2)}) async-start(s8[4718592]{0:T(1024)(128)(4,1)} %bitcast.32), calls=%async_computation.4 | async-start | bytes 8388608
  539.3 6.2 %copy-start.2 = (f32[96,96,16]{2,1,0:T(8,128)S(1)}, f32[96,96,16]{2,1,0:T(8,128)}, u32[]{:S(2)}) copy-start(f32[96,96,16]{2,1,0:T(8,128)} %copy.29) | copy-start | bytes 1769476
  539.3 6.6 %copy-start.3 = (f32[96,16,160]{2,1,0:T(8,128)S(1)}, f32[96,16,160]{2,1,0:T(8,128)}, u32[]{:S(2)}) copy-start(f32[96,16,160]{2,1,0:T(8,128)} %copy.24) | copy-start | bytes 2949124
  539.3 6.9 %copy-start.5 = (f32[16,64,160]{2,1,0:T(8,128)S(1)}, f32[16,64,160]{2,1,0:T(8,128)}, u32[]{:S(2)}) copy-start(f32[16,64,160]{2,1,0:T(8,128)} %copy-done.4) | copy-start | bytes 1966084
Sparse Core Ops, SparseCore 0:
  253.0 40.6 reduce-scatter.1
